TPU v7x, 32 devices: a whole 2x2x4 slice. The times are simulated.
32 devices in a mesh: tok: 8 (over z, y), exp: 4 (over x, core).
Axes of the slice: x: 2, y: 2, z: 4, core: 2. Of those that a mesh axis runs over, the one named last changes fastest.
Arguments:
- tokens: bfloat16 [12, 8192, 1024], P(None, 'tok'), may hold values from -24 to 24
- slot_params: bfloat16 [1024, 128], P(None, 'exp'), may hold values from -2 to 2
- w_in: bfloat16 [64, 1024, 4096], P('exp', None, 'tok'), may hold values from -0.75 to 0.75
- w_out: bfloat16 [64, 4096, 1024], P('exp', 'tok'), may hold values from -0.1875 to 0.1875
Outputs:
- mixed: bfloat16 [12, 8192, 1024], P(None, 'tok', 'exp')
All inputs are finite; a program needn't handle non-finite values.
Results may differ from a plain program's by a relative error of at most 0.0072.
Values may be sent and summed in bfloat16 or wider, within the bound.
A program may use at most 192 MiB of HBM per device.

v0:
```python
import jax
import jax.numpy as jnp
from jax import lax
from jax.sharding import PartitionSpec as P

SLOTS_PER = 2


def shards(tokens, slot_params, w_in, w_out):
    own_width = slot_params.shape[1]
    own_logits = jnp.einsum("std,dj->sjt", tokens, slot_params, preferred_element_type=jnp.float32)
    all_logits = lax.all_gather(own_logits, "exp", axis=1, tiled=True)
    local_max = jnp.max(own_logits, axis=2)
    slot_peak = lax.pmax(local_max, "tok")
    dexp = jnp.exp(own_logits - slot_peak[:, :, None])
    local_den = jnp.sum(dexp, axis=2)
    dweight = dexp.astype(jnp.bfloat16)
    local_sum = jnp.einsum("sjt,std->sjd", dweight, tokens, preferred_element_type=jnp.float32)
    slot_sum, slot_den = lax.psum((local_sum, local_den), "tok")
    slot_in = (slot_sum / slot_den[:, :, None]).astype(jnp.bfloat16)
    seq_count = tokens.shape[0]
    local_experts = w_in.shape[0]
    width = tokens.shape[2]
    grouped = slot_in.reshape(seq_count, local_experts, SLOTS_PER, width)
    hidden = jax.nn.gelu(
        jnp.einsum("sepd,edf->sepf", grouped, w_in, preferred_element_type=jnp.float32),
        approximate=True,
    ).astype(jnp.bfloat16)
    partial_out = jnp.einsum("sepf,efd->sepd", hidden, w_out, preferred_element_type=jnp.float32)
    partial_out = partial_out.reshape(seq_count, own_width, width)
    summed = lax.psum(partial_out, "tok").astype(jnp.bfloat16)
    slot_out = lax.all_to_all(summed, "exp", split_axis=2, concat_axis=1, tiled=True)
    comb_max = jnp.max(all_logits, axis=1)
    cexp = jnp.exp(all_logits - comb_max[:, None, :])
    cweight = (cexp / jnp.sum(cexp, axis=1)[:, None, :]).astype(jnp.bfloat16)
    mixed = jnp.einsum("sjt,sjd->std", cweight, slot_out, preferred_element_type=jnp.float32)
    return mixed.astype(jnp.bfloat16)


def solution(mesh):
    return jax.shard_map(
        shards,
        mesh=mesh,
        in_specs=(
            P(None, "tok", None),
            P(None, "exp"),
            P("exp", None, "tok"),
            P("exp", "tok", None),
        ),
        out_specs=P(None, "tok", "exp"),
        check_vma=False,
    )
```

profile of v0, /device:TPU:0, one launch (start us, length us, event | category | flops | bytes accessed | tf_op | source)
XLA Modules:
  0.0 546.4 jit_solution(2624365932778062341)
XLA Ops:
  7.4 0.8 copy-done
  8.2 12.3 %fusion.28 = (f32[12,32]{1,0:T(8,128)S(1)}, f32[12,32,1024]{2,1,0:T(8,128)S(1)}) fusion(bf16[12,1024,1024]{2,1,0:T(8,128)(2,1)} %param.4, bf16[1024,32]{0,1:T(8,128)(2,1)S(1)} %copy-done), kind=kOutput, calls=%fused_computation.28 | convolution fusion | flops 805699200 | bytes 26805760 | tf_op jit(solution)/shard_map/std,dj->sjt/dot_general | solution.py:11
  20.5 23.4 %pmax.7 = f32[12,32]{1,0:T(8,128)S(1)} all-reduce(f32[12,32]{1,0:T(8,128)S(1)} %get-tuple-element.5), channel_id=1, replica_groups=mesh['tok'=8,'exp'=4] {'tok'}, use_global_device_ids=true, to_apply=%region_3.0 | all-reduce | flops 384 | bytes 3072 | tf_op jit(solution)/shard_map/pmax | solution.py:14
  43.9 11.7 %fusion.23 = f32[12,32,1024]{2,1,0:T(8,128)} fusion(bf16[12,1024,1024]{2,1,0:T(8,128)(2,1)} %param.4, f32[12,32,1024]{2,1,0:T(8,128)S(1)} %get-tuple-element.6, f32[12,32]{1,0:T(8,128)S(1)} %pmax.7), kind=kOutput, calls=%fused_computation.24 | convolution fusion | flops 806092800 | bytes 28313088 | tf_op jit(solution)/shard_map/sjt,std->sjd/dot_general | solution.py:18
  55.6 0.0 all-reduce.3.cloned.1.call-update
  55.6 0.0 all-gather.2.cloned.1.call-start
  55.6 0.5 all-gather.2.cloned.1.call-update
  56.2 1.8 fusion.6
  57.9 18.4 %psum.22 = f32[12,32]{1,0:T(8,128)S(1)} all-reduce(f32[12,32]{1,0:T(8,128)S(1)} %fusion.6), channel_id=1, replica_groups=mesh['tok'=8,'exp'=4] {'tok'}, use_global_device_ids=true, to_apply=%region_6.0 | all-reduce | flops 384 | bytes 3072 | tf_op jit(solution)/shard_map/psum | solution.py:19
  76.3 66.0 %all-reduce.3.cloned.1.call-done = f32[12,32,1024]{2,1,0:T(8,128)} async-done(((f32[12,32,1024]{2,1,0:T(8,128)}), f32[12,32,1024]{2,1,0:T(8,128)}) %all-reduce.3.cloned.1.call-update) | async-done | bytes 1572880 | tf_op jit(solution)/shard_map/psum | solution.py:19
  142.3 1.6 divide_convert_fusion.2
  144.0 0.4 copy.20
  144.4 8.7 %fusion.20 = bf16[12,16,2,512]{3,0,2,1:T(8,128)(2,1)S(1)} fusion(bf16[12,16,2,1024]{3,0,2,1:T(8,128)(2,1)S(1)} %bitcast.48, bf16[16,1024,512]{2,1,0:T(8,128)(2,1)} %param.6), kind=kOutput, calls=%fused_computation.23 | convolution fusion | flops 404422656 | bytes 17956864 | tf_op jit(solution)/shard_map/sepd,edf->sepf/dot_general | solution.py:26
  153.2 8.7 %fusion.1 = f32[16,12,2,1024]{3,1,2,0:T(8,128)S(1)} fusion(bf16[12,16,2,512]{3,0,2,1:T(8,128)(2,1)S(1)} %fusion.20, bf16[16,512,1024]{2,1,0:T(8,128)(2,1)} %param.7), kind=kOutput, calls=%fused_computation.1 | convolution fusion | flops 402653184 | bytes 18743296 | tf_op jit(solution)/shard_map/sepf,efd->sepd/dot_general | solution.py:29
  161.9 6.5 %copy.13 = f32[12,32,1024]{1,0,2:T(8,128)} copy(f32[12,32,1024]{2,0,1:T(8,128)S(1)} %bitcast.47) | data formatting | bytes 3145728 | tf_op jit(solution)/shard_map/reshape | solution.py:30
  168.4 326.7 %all-reduce.4 = bf16[12,32,1024]{1,0,2:T(8,128)(2,1)} all-reduce(f32[12,32,1024]{1,0,2:T(8,128)} %copy.13), channel_id=1, replica_groups=mesh['tok'=8,'exp'=4] {'tok'}, use_global_device_ids=true, to_apply=%region_7.0 | all-reduce | flops 393216 | bytes 2359296 | tf_op jit(solution)/shard_map/psum | solution.py:31
  495.1 5.0 reshape.15
  500.1 14.2 %all_to_all.18 = bf16[4,2,49152]{2,1,0:T(2,128)(2,1)S(1)} all-to-all(bf16[4,2,49152]{2,1,0:T(2,128)(2,1)S(1)} %reshape.15), channel_id=1, replica_groups=mesh['tok'=8,'exp'=4] {'exp'}, dimensions={0} | all-to-all | bytes 1572864 | tf_op jit(solution)/shard_map/all_to_all | solution.py:32
  514.3 4.1 reshape.16
  518.4 5.1 copy.21
  523.6 0.1 copy.15
  523.7 0.0 all-gather.2.cloned.1.call-done
  523.7 5.8 %fusion.29 = f32[12,1024]{1,0:T(8,128)S(1)} fusion(f32[12,128,1024]{2,1,0:T(8,128)} %all-gather.2.cloned.1.call-done), kind=kOutput, calls=%fused_computation.29 | output fusion | flops 3145855 | bytes 6340608 | tf_op jit(solution)/shard_map/sub | solution.py:34
  529.6 9.4 %convolution_convert_fusion = bf16[12,1024,256]{2,1,0:T(8,128)(2,1)} fusion(bf16[12,128,256]{2,1,0:T(8,128)(2,1)S(1)} %bitcast.50, f32[12,1024]{1,0:T(8,128)S(1)} %fusion.29, f32[12,128,1024]{2,1,0:T(8,128)} %all-gather.2.cloned.1.call-done), kind=kOutput, calls=%fused_computation.7 | convolution fusion | flops 813183104 | bytes 13418496 | tf_op jit(solution)/shard_map/sjt,sjd->std/dot_general | solution.py:36
  (6 shorter events, 0.0 us)
Async XLA Ops:
  7.4 0.8 copy-start
  7.4 135.0 %all-reduce.3.cloned.1.call-start = ((), (), s32[]{:S(2)}) async-start(), calls=%async_computation.2 | async-start | bytes 3145728 | tf_op jit(solution)/shard_map/psum | solution.py:19
  20.5 35.0 %copy-start.2 = (f32[12,32,1024]{2,1,0:T(8,128)}, f32[12,32,1024]{2,1,0:T(8,128)S(1)}, u32[]{:S(2)}) copy-start(f32[12,32,1024]{2,1,0:T(8,128)S(1)} %get-tuple-element.6) | copy-start | bytes 4718596
  55.6 468.1 %all-gather.2.cloned.1.call-start = ((), (), s32[]{:S(2)}) async-start(), calls=%async_computation.1 | async-start | bytes 7864320 | tf_op jit(solution)/shard_map/all_gather | solution.py:12
  529.5 9.4 %copy-start.1 = (bf16[1024,32]{0,1:T(8,128)(2,1)S(1)}, bf16[1024,32]{0,1:T(8,128)(2,1)}, u32[]{:S(2)}) copy-start(bf16[1024,32]{0,1:T(8,128)(2,1)} %param.5) | copy-start | bytes 196612
Sparse Core Ops, SparseCore 0:
  55.7 86.5 all-reduce.2
Sparse Core Ops, SparseCore 1:
  57.6 43.5 all-gather.1
where the time goes:
time: 547 us; the launch traced here: 546 us
  blocking collectives  383 us (70%)
  waiting for transfers between devices  66.6 us (12%)
  matrix products  50.8 us (9%)
  local copies, waits for them, and re-layouts  22.2 us (4%)
  between operations  14.9 us (3%)
  other arithmetic  9.19 us (2%)
    psum x1, blocking collectives, shards(): summed = lax.psum(partial_out, 'tok').astype(jnp.bfloat16)  327 us
    psum x1, waiting for transfers between devices, shards(): slot_sum, slot_den = lax.psum((local_sum, local_den), 'tok')  66 us
    pmax x1, blocking collectives, shards(): slot_peak = lax.pmax(local_max, 'tok')  23.4 us
    psum x1, blocking collectives, shards(): slot_sum, slot_den = lax.psum((local_sum, local_den), 'tok')  18.4 us
    all_to_all x1, blocking collectives, shards(): lax.all_to_all(summed, 'exp', split_axis=2, concat_axis=1, tiled=True)  14.2 us
    dot_general x1, matrix products, shards(): jnp.einsum('std,dj->sjt', tokens, slot_params, preferred_element_type=jnp...  12.3 us
    dot_general x1, matrix products, shards(): jnp.einsum('sjt,std->sjd', dweight, tokens, preferred_element_type=jnp.fl...  11.7 us
  transfers between devices with their start and end apart: 2, of which 1 were waited for; matrix products, arithmetic and copies ran while one was open for 8% of the time, Pallas kernels for 0%

commit v1 on v0

--- a/solution.py
+++ b/solution.py
@@ -28,7 +28,7 @@
     ).astype(jnp.bfloat16)
     partial_out = jnp.einsum("sepf,efd->sepd", hidden, w_out, preferred_element_type=jnp.float32)
     partial_out = partial_out.reshape(seq_count, own_width, width)
-    summed = lax.psum(partial_out, "tok").astype(jnp.bfloat16)
+    summed = jnp.sum(lax.all_gather(partial_out, "tok"), axis=0).astype(jnp.bfloat16)
     slot_out = lax.all_to_all(summed, "exp", split_axis=2, concat_axis=1, tiled=True)
     comb_max = jnp.max(all_logits, axis=1)
     cexp = jnp.exp(all_logits - comb_max[:, None, :])

time: 547 us -> 426 us (0.78)
  blocking collectives: 383 us -> 41.5 us
  waiting for transfers between devices: 66.6 us -> 279 us
    psum x1 -> x0, blocking collectives: 327 us -> none  [shards(): summed = lax.psum(partial_out, 'tok').astype(jnp.bfloat16)]
    all_gather x0 -> x1, waiting for transfers between devices: none -> 175 us  [shards(): lax.all_gather(partial_out, 'tok')]
    all_gather x1, waiting for transfers between devices: 0.03 us -> 34.5 us  [shards(): all_logits = lax.all_gather(own_logits, 'exp', axis=1, tiled=True)]
    all_to_all x1 -> x0, blocking collectives: 14.2 us -> none  [shards(): lax.all_to_all(summed, 'exp', split_axis=2, concat_axis=1, tiled=True)]
    reshape x1 -> x0, local copies, waits for them, and re-layouts: 6.51 us -> none  [shards(): partial_out = partial_out.reshape(seq_count, own_width, width)]
    reduce_sum x0 -> x1, other arithmetic: none -> 6.16 us  [shards(): jnp.sum(lax.all_gather(partial_out, 'tok'), axis=0).astype(jnp.bfloat16)]
  transfers between devices with their start and end apart: 2 -> 4, of which waited for: 1 -> 3; matrix products, arithmetic and copies ran while one was open for 8% -> 5% of each run, Pallas kernels for 0% -> 0%
where the time goes in v1:
time: 426 us; the launch traced here: 425 us
  waiting for transfers between devices  279 us (65%)
  matrix products  51 us (12%)
  blocking collectives  41.5 us (10%)
  local copies, waits for them, and re-layouts  23.2 us (5%)
  other arithmetic  14.1 us (3%)
  between operations  13.2 us (3%)
    all_gather x1, waiting for transfers between devices, shards(): lax.all_gather(partial_out, 'tok')  175 us
    psum x1, waiting for transfers between devices, shards(): slot_sum, slot_den = lax.psum((local_sum, local_den), 'tok')  68.3 us
    all_gather x1, waiting for transfers between devices, shards(): all_logits = lax.all_gather(own_logits, 'exp', axis=1, tiled=True)  34.5 us
    pmax x1, blocking collectives, shards(): slot_peak = lax.pmax(local_max, 'tok')  23.4 us
    psum x1, blocking collectives, shards(): slot_sum, slot_den = lax.psum((local_sum, local_den), 'tok')  18.1 us
    dot_general x1, matrix products, shards(): jnp.einsum('std,dj->sjt', tokens, slot_params, preferred_element_type=jnp...  12.3 us
    dot_general x1, matrix products, shards(): jnp.einsum('sjt,std->sjd', dweight, tokens, preferred_element_type=jnp.fl...  11.7 us
    unnamed x8, local copies, waits for them, and re-layouts  10.8 us
  transfers between devices with their start and end apart: 4, of which 3 were waited for; matrix products, arithmetic and copies ran while one was open for 5% of the time, Pallas kernels for 0%

profile of v1, /device:TPU:0, one launch (start us, length us, event | category | flops | bytes accessed | tf_op | source)
XLA Modules:
  0.0 425.3 jit_solution(17810673530607237376)
XLA Ops:
  6.5 0.8 copy-done
  7.4 12.3 %fusion.28 = (f32[12,32]{1,0:T(8,128)S(1)}, f32[12,32,1024]{2,1,0:T(8,128)S(1)}) fusion(bf16[12,1024,1024]{2,1,0:T(8,128)(2,1)} %param.4, bf16[1024,32]{0,1:T(8,128)(2,1)S(1)} %copy-done), kind=kOutput, calls=%fused_computation.28 | convolution fusion | flops 805699200 | bytes 26805760 | tf_op jit(solution)/shard_map/std,dj->sjt/dot_general | solution.py:11
  19.7 23.4 %pmax.7 = f32[12,32]{1,0:T(8,128)S(1)} all-reduce(f32[12,32]{1,0:T(8,128)S(1)} %get-tuple-element.5), channel_id=1, replica_groups=mesh['tok'=8,'exp'=4] {'tok'}, use_global_device_ids=true, to_apply=%region_3.0 | all-reduce | flops 384 | bytes 3072 | tf_op jit(solution)/shard_map/pmax | solution.py:14
  43.1 11.7 %fusion.23 = f32[12,32,1024]{2,1,0:T(8,128)} fusion(bf16[12,1024,1024]{2,1,0:T(8,128)(2,1)} %param.4, f32[12,32,1024]{2,1,0:T(8,128)S(1)} %get-tuple-element.6, f32[12,32]{1,0:T(8,128)S(1)} %pmax.7), kind=kOutput, calls=%fused_computation.24 | convolution fusion | flops 806092800 | bytes 28313088 | tf_op jit(solution)/shard_map/sjt,std->sjd/dot_general | solution.py:18
  54.8 0.4 fusion.6
  55.2 18.1 %psum.15 = f32[12,32]{1,0:T(8,128)S(1)} all-reduce(f32[12,32]{1,0:T(8,128)S(1)} %fusion.6), channel_id=1, replica_groups=mesh['tok'=8,'exp'=4] {'tok'}, use_global_device_ids=true, to_apply=%region_6.0 | all-reduce | flops 384 | bytes 3072 | tf_op jit(solution)/shard_map/psum | solution.py:19
  73.3 68.3 %all-reduce.2.cloned.1.call-done = f32[12,32,1024]{2,1,0:T(8,128)} async-done(((f32[12,32,1024]{2,1,0:T(8,128)}), f32[12,32,1024]{2,1,0:T(8,128)}) %all-reduce.2.cloned.1.call-update) | async-done | bytes 1572880 | tf_op jit(solution)/shard_map/psum | solution.py:19
  141.6 1.6 divide_convert_fusion.2
  143.2 0.4 copy.28
  143.7 8.7 %fusion.20 = bf16[12,16,2,512]{3,0,2,1:T(8,128)(2,1)S(1)} fusion(bf16[12,16,2,1024]{3,0,2,1:T(8,128)(2,1)S(1)} %bitcast.48, bf16[16,1024,512]{2,1,0:T(8,128)(2,1)} %param.6), kind=kOutput, calls=%fused_computation.23 | convolution fusion | flops 404422656 | bytes 17956864 | tf_op jit(solution)/shard_map/sepd,edf->sepf/dot_general | solution.py:26
  152.4 8.7 %fusion.1 = f32[16,12,2,1024]{3,1,2,0:T(8,128)S(1)} fusion(bf16[12,16,2,512]{3,0,2,1:T(8,128)(2,1)S(1)} %fusion.20, bf16[16,512,1024]{2,1,0:T(8,128)(2,1)} %param.7), kind=kOutput, calls=%fused_computation.1 | convolution fusion | flops 402653184 | bytes 18743296 | tf_op jit(solution)/shard_map/sepf,efd->sepd/dot_general | solution.py:29
  161.2 2.1 copy.18
  163.3 0.2 all-gather.3.cloned.1.call-start
  163.5 0.5 all-gather.3.cloned.1.call-update
  164.0 175.2 %all-gather.5.cloned.1.call-done = f32[8,12,32,1024]{3,2,1,0:T(8,128)} async-done(((f32[1,12,32,1024]{3,2,1,0:T(8,128)}), f32[8,12,32,1024]{3,2,1,0:T(8,128)}) %all-gather.5.cloned.1.call-update) | async-done | bytes 12582928 | tf_op jit(solution)/shard_map/all_gather | solution.py:31
  339.3 6.2 %reduce_sum.29 = bf16[12,32,1024]{2,1,0:T(8,128)(2,1)S(1)} reduce(f32[8,12,32,1024]{3,2,1,0:T(8,128)} %all-gather.5.cloned.1.call-done, f32[]{:T(128)} %constant.1.clone.1), dimensions={0}, to_apply=%region_7.0 | reduce | flops 2752512 | bytes 13369348 | tf_op jit(solution)/shard_map/reduce_sum | solution.py:31
  345.4 4.7 %copy.21 = bf16[12,32,1024]{1,0,2:T(8,128)(2,1)} copy(bf16[12,32,1024]{2,1,0:T(8,128)(2,1)S(1)} %reduce_sum.29) | data formatting | bytes 1572864 | tf_op jit(solution)/shard_map/convert_element_type | solution.py:31
  350.1 5.8 %reshape.11 = bf16[4,2,49152]{2,1,0:T(2,128)(2,1)} reshape(bf16[1024,12,32]{2,1,0:T(8,128)(2,1)} %bitcast.45) | data formatting | bytes 1572864
  355.9 3.5 all-to-all-start
  359.4 34.5 %all-gather.3.cloned.1.call-done = f32[12,128,1024]{2,1,0:T(8,128)} async-done(((f32[12,32,1024]{2,1,0:T(8,128)}), f32[12,128,1024]{2,1,0:T(8,128)}) %all-gather.3.cloned.1.call-update) | async-done | bytes 6291472 | tf_op jit(solution)/shard_map/all_gather | solution.py:12
  393.8 6.0 %fusion.29 = f32[12,1024]{1,0:T(8,128)S(1)} fusion(f32[12,128,1024]{2,1,0:T(8,128)} %all-gather.3.cloned.1.call-done), kind=kOutput, calls=%fused_computation.29 | output fusion | flops 3145855 | bytes 6340608 | tf_op jit(solution)/shard_map/sub | solution.py:34
  399.8 4.1 reshape.12
  404.0 5.1 %copy.29 = bf16[12,32,4,256]{3,2,1,0:T(4,128)(2,1)S(1)} copy(bf16[12,32,4,256]{1,0,3,2:T(8,128)(2,1)} %bitcast.46) | data formatting | bytes 1572864 | tf_op jit(solution)/shard_map/all_to_all | solution.py:32
  409.2 9.5 %convolution_convert_fusion = bf16[12,1024,256]{2,1,0:T(8,128)(2,1)} fusion(bf16[12,128,256]{2,1,0:T(8,128)(2,1)S(1)} %bitcast.50, f32[12,1024]{1,0:T(8,128)S(1)} %fusion.29, f32[12,128,1024]{2,1,0:T(8,128)} %all-gather.3.cloned.1.call-done), kind=kOutput, calls=%fused_computation.7 | convolution fusion | flops 813183104 | bytes 13418496 | tf_op jit(solution)/shard_map/sjt,sjd->std/dot_general | solution.py:36
  (11 shorter events, 0.2 us)
Async XLA Ops:
  6.5 0.8 copy-start
  6.5 135.1 %all-reduce.2.cloned.1.call-start = ((), (), s32[]{:S(2)}) async-start(), calls=%async_computation.2 | async-start | bytes 3145728 | tf_op jit(solution)/shard_map/psum | solution.py:19
  19.7 35.1 %copy-start.2 = (f32[12,32,1024]{2,1,0:T(8,128)}, f32[12,32,1024]{2,1,0:T(8,128)S(1)}, u32[]{:S(2)}) copy-start(f32[12,32,1024]{2,1,0:T(8,128)S(1)} %get-tuple-element.6) | copy-start | bytes 4718596
  54.7 284.5 %all-gather.5.cloned.1.call-start = ((), (), s32[]{:S(2)}) async-start(), calls=%async_computation.3 | async-start | bytes 14155776 | tf_op jit(solution)/shard_map/all_gather | solution.py:31
  163.3 230.6 %all-gather.3.cloned.1.call-start = ((), (), s32[]{:S(2)}) async-start(), calls=%async_computation.1 | async-start | bytes 7864320 | tf_op jit(solution)/shard_map/all_gather | solution.py:12
  355.9 43.9 %all-to-all-start = ((bf16[4,2,49152]{2,1,0:T(2,128)(2,1)}), bf16[4,2,49152]{2,1,0:T(2,128)(2,1)S(1)}, u32[]{:S(2)}, u32[]{:S(2)}) async-start(bf16[4,2,49152]{2,1,0:T(2,128)(2,1)} %reshape.11), calls=%async_computation | async-start | bytes 1572864 | tf_op jit(solution)/shard_map/all_to_all | solution.py:32
  409.2 9.6 %copy-start.1 = (bf16[1024,32]{0,1:T(8,128)(2,1)S(1)}, bf16[1024,32]{0,1:T(8,128)(2,1)}, u32[]{:S(2)}) copy-start(bf16[1024,32]{0,1:T(8,128)(2,1)} %param.5) | copy-start | bytes 196612
Sparse Core Ops, SparseCore 0:
  54.9 86.7 all-reduce.1
  163.4 175.8 all-gather.4
  340.8 52.9 all-gather.2
